TPU v7x, 32 devices: a whole 2x2x4 slice. The times are simulated.
32 devices in a mesh: fsdp: 4 (over z), ctx: 4 (over x, core), tp: 2 (over y).
Axes of the slice: x: 2, y: 2, z: 4, core: 2. Of those that a mesh axis runs over, the one named last changes fastest.
Arguments:
- x_in: bfloat16 [8, 1024, 2048], P(None, ('fsdp', 'ctx')), may hold values from -6 to 6
- cotangent: bfloat16 [8, 1024, 2048], P(None, ('fsdp', 'ctx')), may hold values from -6 to 6
- lengths: int32 [8], replicated, may hold values from 128 to 1024, as said below
- adapter_ids: int32 [8], replicated, may hold values from 0 to 7
- w_qkv: bfloat16 [3, 2048, 2048], P(None, 'fsdp', 'tp'), may hold values from -0.125 to 0.125
- w_out: bfloat16 [2048, 2048], P('tp', 'fsdp'), may hold values from -2 to 2
- w_up: bfloat16 [2048, 8192], P('fsdp', 'tp'), may hold values from -0.125 to 0.125
- w_down: bfloat16 [8192, 2048], P('tp', 'fsdp'), may hold values from -0.0625 to 0.0625
- ln_gain: float32 [2, 2048], replicated, may hold values from 0.1 to 1.9
- ln_bias: float32 [2, 2048], replicated, may hold values from -1.5 to 1.5
- a_qkv: bfloat16 [3, 2048, 128], replicated, may hold values from -0.125 to 0.125
- b_qkv: bfloat16 [3, 128, 2048], P(None, None, 'tp'), may hold values from -0.5 to 0.5
- a_out: bfloat16 [2048, 128], P('tp'), may hold values from -2 to 2
- b_out: bfloat16 [128, 2048], replicated, may hold values from -0.5 to 0.5
- a_up: bfloat16 [2048, 128], replicated, may hold values from -0.125 to 0.125
- b_up: bfloat16 [128, 8192], P(None, 'tp'), may hold values from -0.5 to 0.5
- a_down: bfloat16 [8192, 128], P('tp'), may hold values from -0.0625 to 0.0625
- b_down: bfloat16 [128, 2048], replicated, may hold values from -0.5 to 0.5
Outputs:
- activations: bfloat16 [8, 1024, 2048], P(None, ('fsdp', 'ctx'))
- input_grad: bfloat16 [8, 1024, 2048], P(None, ('fsdp', 'ctx'))
- grad_a_qkv: float32 [3, 2048, 128], replicated
- grad_b_qkv: float32 [3, 128, 2048], P(None, None, 'tp')
- grad_a_out: float32 [2048, 128], P('tp')
- grad_b_out: float32 [128, 2048], replicated
- grad_a_up: float32 [2048, 128], replicated
- grad_b_up: float32 [128, 8192], P(None, 'tp')
- grad_a_down: float32 [8192, 128], P('tp')
- grad_b_down: float32 [128, 2048], replicated
Inputs may be any that keep to these rules, and one draw needn't show every extreme that they name: `lengths`: each aligned block of 2 sequences holds at least one sequence of length 1024.
All inputs are finite; a program needn't handle non-finite values.
Results may differ from a plain program's by a relative error of at most 0.019.
Values may be sent and summed in bfloat16 or wider, within the bound.
A program may use at most 256 MiB of HBM per device.

v0:
```python
from functools import partial
import math
import jax
import jax.numpy as jnp
from jax import lax
from jax.sharding import PartitionSpec as P

HEAD_DIM = 128
RANK = 16
ADAPTERS = 8
NORM_EPS = 1e-06
GELU_COEF = 0.7978845608028654


def norm_rows(values, gain_row, shift_row):
    center = values - jnp.mean(values, axis=-1, keepdims=True)
    spread = jnp.mean(center * center, axis=-1, keepdims=True)
    return center * lax.rsqrt(spread + NORM_EPS) * gain_row + shift_row


def gelu_tanh(values):
    return (
        0.5 * values * (1.0 + jnp.tanh(GELU_COEF * (values + 0.044715 * values * values * values)))
    )


def product(left_side, right_side):
    return jnp.dot(left_side, right_side, preferred_element_type=jnp.float32)


def against(left_side, right_side):
    return lax.dot_general(
        left_side, right_side, (((1,), (1,)), ((), ())), preferred_element_type=jnp.float32
    )


def across(left_side, right_side):
    return lax.dot_general(
        left_side, right_side, (((0,), (0,)), ((), ())), preferred_element_type=jnp.float32
    )


def local(
    x_in,
    cotangent,
    lengths,
    adapter_ids,
    w_qkv,
    w_out,
    w_up,
    w_down,
    ln_gain,
    ln_bias,
    a_qkv,
    b_qkv,
    a_out,
    b_out,
    a_up,
    b_up,
    a_down,
    b_down,
):
    n_ctx = lax.axis_size("ctx")
    n_fsdp = lax.axis_size("fsdp")
    owner_index = lax.axis_index("fsdp")
    seq_total, piece_rows, model_width = x_in.shape
    per_dev = seq_total // n_fsdp
    local_len = n_fsdp * piece_rows
    dev_rows = per_dev * local_len
    key_count = n_ctx * local_len
    heads_width = w_qkv.shape[2]
    heads_here = heads_width // HEAD_DIM
    score_scale = 1.0 / math.sqrt(HEAD_DIM)
    dealt_x, dealt_cot = (
        lax.all_to_all(x_in, "fsdp", split_axis=0, concat_axis=1, tiled=True),
        lax.all_to_all(cotangent, "fsdp", split_axis=0, concat_axis=1, tiled=True),
    )
    x_rows = dealt_x.reshape(dev_rows, model_width)
    my_lengths = lax.dynamic_slice_in_dim(lengths, owner_index * per_dev, per_dev)
    my_ids = lax.dynamic_slice_in_dim(adapter_ids, owner_index * per_dev, per_dev)
    picked = (my_ids[:, None] == jnp.arange(ADAPTERS)[None, :]).astype(jnp.float32)
    pick_rows = jnp.repeat(jnp.repeat(picked, RANK, axis=1), local_len, axis=0)
    key_index = jnp.arange(key_count)
    ctx_block = key_index // local_len
    remain = key_index % local_len
    key_pos = (remain // piece_rows * n_ctx + ctx_block) * piece_rows + remain % piece_rows
    usable = key_pos[None, :] < my_lengths[:, None]
    qkv_full, out_full = (
        lax.all_gather(w_qkv, "fsdp", axis=1, tiled=True),
        lax.all_gather(w_out, "fsdp", axis=1, tiled=True),
    )
    adapt_qkv = [
        (product(x_rows, a_qkv[proj_index]) * pick_rows).astype(jnp.bfloat16)
        for proj_index in range(3)
    ]
    projected = [
        (product(x_rows, qkv_full[proj_index]) + product(adapt_qkv[proj_index], b_qkv[proj_index]))
        .astype(jnp.bfloat16)
        .reshape(per_dev, local_len, heads_width)
        for proj_index in range(3)
    ]
    queries_all = projected[0]
    keys_all, values_all = (
        lax.all_gather(projected[1], "ctx", axis=1, tiled=True),
        lax.all_gather(projected[2], "ctx", axis=1, tiled=True),
    )

    def score_block(query_heads, key_heads, usable_row):
        scores = (
            jnp.einsum("qhd,khd->hqk", query_heads, key_heads, preferred_element_type=jnp.float32)
            * score_scale
        )
        return jnp.where(usable_row[None, None, :], scores, -1e30)

    def attend(packed):
        queries, keys_seq, values_seq, usable_row = packed
        query_heads = queries.reshape(local_len, heads_here, HEAD_DIM)
        key_heads = keys_seq.reshape(key_count, heads_here, HEAD_DIM)
        value_heads = values_seq.reshape(key_count, heads_here, HEAD_DIM)
        scores = score_block(query_heads, key_heads, usable_row)
        row_max = jnp.max(scores, axis=-1, keepdims=True)
        row_total = jnp.sum(jnp.exp(scores - row_max), axis=-1, keepdims=True)
        log_total = row_max + jnp.log(row_total)
        attn_probs = jnp.exp(scores - log_total).astype(jnp.bfloat16)
        mixed_heads = jnp.einsum(
            "hqk,khd->qhd", attn_probs, value_heads, preferred_element_type=jnp.float32
        )
        return (mixed_heads.reshape(local_len, heads_width).astype(jnp.bfloat16), log_total[..., 0])

    context, log_totals = lax.map(attend, (queries_all, keys_all, values_all, usable))
    ctx_rows = context.reshape(dev_rows, heads_width)
    part_out = product(ctx_rows, out_full)
    part_adapt = product(ctx_rows, a_out) * pick_rows
    attn_sum, adapt_out_sum = lax.psum((part_out, part_adapt), "tp")
    adapt_out = adapt_out_sum.astype(jnp.bfloat16)
    attn_branch = attn_sum + product(adapt_out, b_out)
    hidden_one, norm_one_back = jax.vjp(
        partial(norm_rows, gain_row=ln_gain[0], shift_row=ln_bias[0]),
        x_rows.astype(jnp.float32) + attn_branch,
    )
    hidden_low = hidden_one.astype(jnp.bfloat16)
    up_full, down_full = (
        lax.all_gather(w_up, "fsdp", axis=0, tiled=True),
        lax.all_gather(w_down, "fsdp", axis=1, tiled=True),
    )
    adapt_up = (product(hidden_low, a_up) * pick_rows).astype(jnp.bfloat16)
    pre_act = product(hidden_low, up_full) + product(adapt_up, b_up)
    activated, gelu_back = jax.vjp(gelu_tanh, pre_act)
    gelu_out = activated.astype(jnp.bfloat16)
    part_down = product(gelu_out, down_full)
    part_adapt_down = product(gelu_out, a_down) * pick_rows
    down_sum, adapt_down_sum = lax.psum((part_down, part_adapt_down), "tp")
    adapt_down = adapt_down_sum.astype(jnp.bfloat16)
    second_in = hidden_one + down_sum + product(adapt_down, b_down)
    layer_out, norm_two_back = jax.vjp(
        partial(norm_rows, gain_row=ln_gain[1], shift_row=ln_bias[1]), second_in
    )
    grad_out = dealt_cot.reshape(dev_rows, model_width).astype(jnp.float32)
    (grad_second,) = norm_two_back(grad_out)
    grad_down_low = grad_second.astype(jnp.bfloat16)
    up_back, down_back = (
        lax.all_gather(w_up, "fsdp", axis=0, tiled=True),
        lax.all_gather(w_down, "fsdp", axis=1, tiled=True),
    )
    grad_adapt_down = (against(grad_down_low, b_down) * pick_rows).astype(jnp.bfloat16)
    grad_b_down = across(adapt_down, grad_down_low)
    grad_a_down = across(gelu_out, grad_adapt_down)
    grad_gelu = against(grad_down_low, down_back) + against(grad_adapt_down, a_down)
    (grad_pre,) = gelu_back(grad_gelu)
    grad_pre_low = grad_pre.astype(jnp.bfloat16)
    grad_b_up = across(adapt_up, grad_pre_low)
    part_hidden = against(grad_pre_low, up_back)
    part_adapt_up = against(grad_pre_low, b_up)
    grad_hidden_sum, grad_adapt_up_sum = lax.psum((part_hidden, part_adapt_up), "tp")
    grad_adapt_up = (grad_adapt_up_sum * pick_rows).astype(jnp.bfloat16)
    grad_a_up = across(hidden_low, grad_adapt_up)
    grad_hidden = grad_second + grad_hidden_sum + against(grad_adapt_up, a_up)
    (grad_first,) = norm_one_back(grad_hidden)
    grad_attn_low = grad_first.astype(jnp.bfloat16)
    qkv_back, out_back = (
        lax.all_gather(w_qkv, "fsdp", axis=1, tiled=True),
        lax.all_gather(w_out, "fsdp", axis=1, tiled=True),
    )
    grad_adapt_out = (against(grad_attn_low, b_out) * pick_rows).astype(jnp.bfloat16)
    grad_b_out = across(adapt_out, grad_attn_low)
    grad_a_out = across(ctx_rows, grad_adapt_out)
    grad_context = (against(grad_attn_low, out_back) + against(grad_adapt_out, a_out)).astype(
        jnp.bfloat16
    )

    def attend_back(packed):
        queries, keys_seq, values_seq, usable_row, log_total, grad_ctx_seq = packed
        query_heads = queries.reshape(local_len, heads_here, HEAD_DIM)
        key_heads = keys_seq.reshape(key_count, heads_here, HEAD_DIM)
        value_heads = values_seq.reshape(key_count, heads_here, HEAD_DIM)
        scores = score_block(query_heads, key_heads, usable_row)
        attn_probs = jnp.exp(scores - log_total[..., None])
        probs_low = attn_probs.astype(jnp.bfloat16)
        grad_heads = grad_ctx_seq.reshape(local_len, heads_here, HEAD_DIM)
        grad_values = jnp.einsum(
            "hqk,qhd->khd", probs_low, grad_heads, preferred_element_type=jnp.float32
        )
        grad_probs = jnp.einsum(
            "qhd,khd->hqk", grad_heads, value_heads, preferred_element_type=jnp.float32
        )
        row_dot = jnp.sum(attn_probs * grad_probs, axis=-1, keepdims=True)
        grad_scores = (attn_probs * (grad_probs - row_dot)).astype(jnp.bfloat16)
        grad_query = (
            jnp.einsum("hqk,khd->qhd", grad_scores, key_heads, preferred_element_type=jnp.float32)
            * score_scale
        )
        grad_keys = (
            jnp.einsum("hqk,qhd->khd", grad_scores, query_heads, preferred_element_type=jnp.float32)
            * score_scale
        )
        return (
            grad_query.reshape(local_len, heads_width).astype(jnp.bfloat16),
            grad_keys.reshape(key_count, heads_width),
            grad_values.reshape(key_count, heads_width),
        )

    grad_ctx_seqs = grad_context.reshape(per_dev, local_len, heads_width)
    grad_queries, grad_keys_all, grad_values_all = lax.map(
        attend_back, (queries_all, keys_all, values_all, usable, log_totals, grad_ctx_seqs)
    )
    grad_keys_mine, grad_values_mine = (
        lax.psum_scatter(
            grad_keys_all.astype(jnp.bfloat16), "ctx", scatter_dimension=1, tiled=True
        ).astype(jnp.float32),
        lax.psum_scatter(
            grad_values_all.astype(jnp.bfloat16), "ctx", scatter_dimension=1, tiled=True
        ).astype(jnp.float32),
    )
    grad_proj = [
        grad_queries.reshape(dev_rows, heads_width),
        grad_keys_mine.astype(jnp.bfloat16).reshape(dev_rows, heads_width),
        grad_values_mine.astype(jnp.bfloat16).reshape(dev_rows, heads_width),
    ]
    grad_b_qkv = jnp.stack(
        [across(adapt_qkv[proj_index], grad_proj[proj_index]) for proj_index in range(3)]
    )
    part_input = (
        against(grad_proj[0], qkv_back[0])
        + against(grad_proj[1], qkv_back[1])
        + against(grad_proj[2], qkv_back[2])
    )
    part_adapt_qkv = jnp.stack(
        [against(grad_proj[proj_index], b_qkv[proj_index]) for proj_index in range(3)]
    )
    grad_input_sum, grad_adapt_qkv_sum = (
        lax.psum(part_input.astype(jnp.bfloat16), "tp").astype(jnp.float32),
        lax.psum(part_adapt_qkv.astype(jnp.bfloat16), "tp").astype(jnp.float32),
    )
    grad_adapt_qkv = (grad_adapt_qkv_sum * pick_rows[None]).astype(jnp.bfloat16)
    grad_a_qkv = jnp.stack([across(x_rows, grad_adapt_qkv[proj_index]) for proj_index in range(3)])
    grad_input = (
        grad_first
        + grad_input_sum
        + against(grad_adapt_qkv[0], a_qkv[0])
        + against(grad_adapt_qkv[1], a_qkv[1])
        + against(grad_adapt_qkv[2], a_qkv[2])
    )
    summed_grads = lax.psum(
        (
            grad_a_qkv,
            grad_b_qkv,
            grad_a_out,
            grad_b_out,
            grad_a_up,
            grad_b_up,
            grad_a_down,
            grad_b_down,
        ),
        ("fsdp", "ctx"),
    )
    out_low = layer_out.astype(jnp.bfloat16).reshape(per_dev, local_len, model_width)
    input_low = grad_input.astype(jnp.bfloat16).reshape(per_dev, local_len, model_width)
    back_out, back_input = (
        lax.all_to_all(out_low, "fsdp", split_axis=1, concat_axis=0, tiled=True),
        lax.all_to_all(input_low, "fsdp", split_axis=1, concat_axis=0, tiled=True),
    )
    return (
        back_out,
        back_input,
        summed_grads[0],
        summed_grads[1],
        summed_grads[2],
        summed_grads[3],
        summed_grads[4],
        summed_grads[5],
        summed_grads[6],
        summed_grads[7],
    )


def solution(mesh):
    return jax.shard_map(
        local,
        mesh=mesh,
        in_specs=(
            P(None, ("fsdp", "ctx"), None),
            P(None, ("fsdp", "ctx"), None),
            P(),
            P(),
            P(None, "fsdp", "tp"),
            P("tp", "fsdp"),
            P("fsdp", "tp"),
            P("tp", "fsdp"),
            P(),
            P(),
            P(),
            P(None, None, "tp"),
            P("tp", None),
            P(),
            P(),
            P(None, "tp"),
            P("tp", None),
            P(),
        ),
        out_specs=(
            P(None, ("fsdp", "ctx"), None),
            P(None, ("fsdp", "ctx"), None),
            P(),
            P(None, None, "tp"),
            P("tp", None),
            P(),
            P(),
            P(None, "tp"),
            P("tp", None),
            P(),
        ),
        check_vma=False,
    )
```

profile of v0, /device:TPU:0, one launch (start us, length us, event | category | flops | bytes accessed | tf_op | source)
XLA Modules:
  0.0 2011.4 jit_solution(7236679362293835580)
XLA Ops:
  14.6 104.2 %all-to-all-done = bf16[8,64,2048]{2,1,0:T(8,128)(2,1)S(1)} async-done(((bf16[8,64,2048]{2,1,0:T(8,128)(2,1)}), bf16[8,64,2048]{2,1,0:T(8,128)(2,1)S(1)}, u32[]{:S(2)}, u32[]{:S(2)}) %all-to-all-start) | async-done | bytes 2097184 | tf_op jit(solution)/shard_map/all_to_all | solution.py:75
  124.0 141.4 %all-gather.7.cloned.1.call-done = bf16[3,2048,1024]{2,1,0:T(8,128)(2,1)} async-done(((bf16[3,512,1024]{2,1,0:T(8,128)(2,1)}), bf16[3,2048,1024]{2,1,0:T(8,128)(2,1)}) %all-gather.7.cloned.1.call-update) | async-done | bytes 12582928 | tf_op jit(solution)/shard_map/all_gather | solution.py:89
  297.6 11.3 all-gather.11.cloned.1.call-done
  308.8 37.2 %all-gather.9.cloned.1.call-done = bf16[2,1024,1024]{1,2,0:T(8,128)(2,1)} async-done(((bf16[2,256,1024]{1,2,0:T(8,128)(2,1)}), bf16[2,1024,1024]{1,2,0:T(8,128)(2,1)}) %all-gather.9.cloned.1.call-update) | async-done | bytes 4194320 | tf_op jit(solution)/shard_map/all_gather | solution.py:105
  347.1 26.9 %while.26 = (s32[]{:T(128)}, bf16[2,256,1024]{2,1,0:T(8,128)(2,1)}, f32[2,8,256]{2,1,0:T(8,128)S(1)}, bf16[2,1024,1024]{1,2,0:T(8,128)(2,1)}, pred[2,1024]{1,0:T...) while((s32[]{:T(128)}, bf16[2,256,1024]{2,1,0:T(8,128)(2,1)}, ...), condition=%wide.region_3.4_spmd, body=%wide.region_0.3_spmd.sunk | while | flops 1097070592 | bytes 46208640 | solution.py:130
  374.1 54.2 %all-gather.13.cloned.1.call-done = bf16[1024,2048]{1,0:T(8,128)(2,1)} async-done(((bf16[1024,512]{1,0:T(8,128)(2,1)}), bf16[1024,2048]{1,0:T(8,128)(2,1)}) %all-gather.13.cloned.1.call-update) | async-done | bytes 4194320 | tf_op jit(solution)/shard_map/all_gather | solution.py:90
  439.0 19.6 all-reduce.20
  458.6 88.7 %all-reduce.11.cloned.1.call-done = f32[512,2048]{1,0:T(8,128)} async-done(((f32[512,2048]{1,0:T(8,128)}), f32[512,2048]{1,0:T(8,128)}) %all-reduce.11.cloned.1.call-update) | async-done | bytes 4194320 | tf_op jit(solution)/shard_map/psum | solution.py:134
  559.5 276.1 %all-gather.15.cloned.1.call-done = bf16[2048,4096]{1,0:T(8,128)(2,1)} async-done(((bf16[512,4096]{1,0:T(8,128)(2,1)}), bf16[2048,4096]{1,0:T(8,128)(2,1)}) %all-gather.15.cloned.1.call-update) | async-done | bytes 16777232 | tf_op jit(solution)/shard_map/all_gather | solution.py:143
  835.6 20.4 %multiply_convert_fusion.1 = (bf16[512,4096]{1,0:T(8,128)(2,1)}, f32[512,4096]{1,0:T(8,128)}) fusion(f32[512,4096]{1,0:T(8,128)} %fusion.102, bf16[512,2048]{1,0:T(8,128)(2,1)S(1)} %fusion.31, bf16[2048,4096]{1,0:T(8,128)(2,1)} %all-gather.15.cloned.1.call-done), kind=kOutput, calls=%fused_computation.52 | convolution fusion | flops 8610906112 | bytes 39845888 | tf_op jit(solution)/shard_map/dot_general | solution.py:28
  856.0 266.2 %all-gather.17.cloned.1.call-done = bf16[4096,2048]{1,0:T(8,128)(2,1)} async-done(((bf16[4096,512]{1,0:T(8,128)(2,1)}), bf16[4096,2048]{1,0:T(8,128)(2,1)}) %all-gather.17.cloned.1.call-update) | async-done | bytes 16777232 | tf_op jit(solution)/shard_map/all_gather | solution.py:144
  1122.2 14.9 fusion.103
  1138.7 51.1 %all_to_all.60 = bf16[8,64,2048]{2,1,0:T(8,128)(2,1)S(1)} all-to-all(bf16[8,64,2048]{2,1,0:T(8,128)(2,1)S(1)} %copy-done.39), channel_id=1, replica_groups=mesh['fsdp'=4,'ctx'=4,'tp'=2] {'fsdp'}, dimensions={0} | all-to-all | bytes 4194304 | tf_op jit(solution)/shard_map/all_to_all | solution.py:76
  1194.8 18.6 all-reduce.21
  1213.4 35.5 %all-reduce.13.cloned.1.call-done = f32[512,2048]{1,0:T(8,128)} async-done(((f32[512,2048]{1,0:T(8,128)}), f32[512,2048]{1,0:T(8,128)}) %all-reduce.13.cloned.1.call-update) | async-done | bytes 4194320 | tf_op jit(solution)/shard_map/psum | solution.py:152
  1264.7 22.3 %fusion.22 = bf16[512,4096]{1,0:T(8,128)(2,1)} fusion(f32[512,4096]{1,0:T(8,128)} %get-tuple-element.250, f32[512,4096]{1,0:T(8,128)} %fusion.104, bf16[512,2048]{1,0:T(8,128)(2,1)S(1)} %add_convert_fusion.4, bf16[4096,2048]{1,0:T(8,128)(2,1)} %all-gather.17.cloned.1.call-done), kind=kOutput, calls=%fused_computation.49 | convolution fusion | flops 8642363392 | bytes 39845888 | tf_op jit(solution)/shard_map/dot_general | solution.py:32
  1291.3 14.0 fusion.105
  1305.4 113.3 %all-reduce.17.cloned.1.call-done = (f32[512,2048]{1,0:T(8,128)}, f32[512,128]{1,0:T(8,128)}) async-done(((f32[512,2048]{1,0:T(8,128)}, f32[512,128]{1,0:T(8,128)}), (f32[512,2048]{1,0:T(8,128)}, f32[512,128]{1,0:T(8,128)})) %all-reduce.17.cloned.1.call-update) | async-done | bytes 4456464 | tf_op jit(solution)/shard_map/psum | solution.py:174
  1436.4 91.7 %while.27 = (s32[]{:T(128)}, bf16[2,256,1024]{2,1,0:T(8,128)(2,1)}, bf16[2,1024,1024]{2,1,0:T(8,128)(2,1)}, bf16[2,1024,1024]{2,1,0:T(8,128)(2,1)}, bf16[2,1024,...) while((s32[]{:T(128)}, bf16[2,256,1024]{2,1,0:T(8,128)(2,1)}, ...), condition=%wide.region_20.21_spmd, body=%wide.region_18.20_spmd.sunk | while | flops 2718431232 | bytes 173603120 | solution.py:223
  1545.5 27.2 %reduce-scatter.3.cloned.1.call-done = bf16[2,256,1024]{2,1,0:T(8,128)(2,1)} async-done(((bf16[2,1024,1024]{2,1,0:T(8,128)(2,1)}), bf16[2,256,1024]{2,1,0:T(8,128)(2,1)}) %reduce-scatter.3.cloned.1.call-update) | async-done | bytes 1048592 | tf_op jit(solution)/shard_map/reduce_scatter | solution.py:227
  1574.4 45.4 %reduce-scatter.5.cloned.1.call-done = bf16[2,256,1024]{2,1,0:T(8,128)(2,1)} async-done(((bf16[2,1024,1024]{2,1,0:T(8,128)(2,1)}), bf16[2,256,1024]{2,1,0:T(8,128)(2,1)}) %reduce-scatter.5.cloned.1.call-update) | async-done | bytes 1048592 | tf_op jit(solution)/shard_map/reduce_scatter | solution.py:230
  1649.0 56.3 %all-reduce.19.cloned.1.call-done = (bf16[3,512,128]{2,1,0:T(8,128)(2,1)}, bf16[512,2048]{1,0:T(8,128)(2,1)}) async-done(((bf16[3,512,128]{2,1,0:T(8,128)(2,1)}, bf16[512,2048]{1,0:T(8,128)(2,1)}), (bf16[3,512,128]{2,1,0:T(8,128)(2,1)}, bf16[512,2048]{1,0:T(8,128)(2,1)})) %all-reduce.19.cloned.1.call-update) | async-done | bytes 2490384 | tf_op jit(solution)/shard_map/psum | solution.py:252
  1727.2 67.8 %all-to-all-done.3 = bf16[2,256,2048]{2,0,1:T(2,128)(2,1)S(1)} async-done(((bf16[2,256,2048]{2,0,1:T(2,128)(2,1)}), bf16[2,256,2048]{2,0,1:T(2,128)(2,1)S(1)}, u32[]{:S(2)}, u32[]{:S(2)}) %all-to-all-start.3) | async-done | bytes 2097184 | tf_op jit(solution)/shard_map/all_to_all | solution.py:280
  1797.2 196.3 %all-reduce.15.cloned.1.call-done = (f32[3,2048,128]{1,2,0:T(8,128)}, f32[3,128,1024]{2,1,0:T(8,128)}, f32[1024,128]{1,0:T(8,128)}, f32[128,2048]{1,0:T(8,128)},...) async-done(((f32[3,2048,128]{1,2,0:T(8,128)}, f32[3,128,1024]{2,1,0:T(8,128)}, f32[1024,128]{1,0:T(8,128)}, ...) | async-done | bytes 12582928 | tf_op jit(solution)/shard_map/psum | solution.py:263
  (365 shorter events, 313.9 us)
Async XLA Ops:
  7.2 1185.3 %copy-start = (bf16[4096,128]{1,0:T(8,128)(2,1)S(1)}, bf16[4096,128]{1,0:T(8,128)(2,1)}, u32[]{:S(2)}) copy-start(bf16[4096,128]{1,0:T(8,128)(2,1)} %param.38) | copy-start | bytes 3145732
  7.2 258.2 %all-gather.7.cloned.1.call-start = ((), (), s32[]{:S(2)}) async-start(), calls=%async_computation.6 | async-start | bytes 15728640 | tf_op jit(solution)/shard_map/all_gather | solution.py:89
  7.9 110.8 %all-to-all-start = ((bf16[8,64,2048]{2,1,0:T(8,128)(2,1)}), bf16[8,64,2048]{2,1,0:T(8,128)(2,1)S(1)}, u32[]{:S(2)}, u32[]{:S(2)}) async-start(bf16[8,64,2048]{2,1,0:T(8,128)(2,1)} %param.22), calls=%async_computation | async-start | bytes 4194304 | tf_op jit(solution)/shard_map/all_to_all | solution.py:75
  14.3 294.6 %all-gather.11.cloned.1.call-start = ((), (), s32[]{:S(2)}) async-start(), calls=%async_computation.8 | async-start | bytes 5242880 | tf_op jit(solution)/shard_map/all_gather | solution.py:104
  14.6 1413.2 %copy-start.71 = (f32[2,128]{1,0:T(2,128)}, f32[2,128]{1,0:T(2,128)S(1)}, u32[]{:S(2)}) copy-start(f32[2,128]{1,0:T(2,128)S(1)} %reshape.257) | copy-start | bytes 3076
  121.8 425.5 %copy-start.6 = (bf16[4,2,64,2048]{3,2,0,1:T(8,128)(2,1)}, bf16[4,2,64,2048]{3,2,0,1:T(8,128)(2,1)S(1)}, u32[]{:S(2)}) copy-start(bf16[4,2,64,2048]{3,2,0,1:T(8,128)(2,1)S(1)} %copy.63) | copy-start | bytes 6291460
  124.0 145.9 %copy-start.53 = (bf16[512,128]{1,0:T(8,128)(2,1)}, bf16[512,128]{1,0:T(8,128)(2,1)S(1)}, u32[]{:S(2)}) copy-start(bf16[512,128]{1,0:T(8,128)(2,1)S(1)} %fusion.34) | copy-start | bytes 393220
  274.5 71.5 %all-gather.9.cloned.1.call-start = ((), (), s32[]{:S(2)}) async-start(), calls=%async_computation.7 | async-start | bytes 5242880 | tf_op jit(solution)/shard_map/all_gather | solution.py:105
  285.6 142.6 %all-gather.13.cloned.1.call-start = ((), (), s32[]{:S(2)}) async-start(), calls=%async_computation.9 | async-start | bytes 5242880 | tf_op jit(solution)/shard_map/all_gather | solution.py:90
  286.2 261.1 %all-reduce.11.cloned.1.call-start = ((), (), s32[]{:S(2)}) async-start(), calls=%async_computation.10 | async-start | bytes 8388608 | tf_op jit(solution)/shard_map/psum | solution.py:134
  374.1 61.0 %copy-start.73 = (f32[2,8,256]{2,1,0:T(8,128)}, f32[2,8,256]{2,1,0:T(8,128)S(1)}, u32[]{:S(2)}) copy-start(f32[2,8,256]{2,1,0:T(8,128)S(1)} %get-tuple-element.410) | copy-start | bytes 49156
  435.1 400.5 %all-gather.15.cloned.1.call-start = ((), (), s32[]{:S(2)}) async-start(), calls=%async_computation.11 | async-start | bytes 20971520 | tf_op jit(solution)/shard_map/all_gather | solution.py:143
  435.7 686.5 %all-gather.17.cloned.1.call-start = ((), (), s32[]{:S(2)}) async-start(), calls=%async_computation.12 | async-start | bytes 20971520 | tf_op jit(solution)/shard_map/all_gather | solution.py:144
  436.5 812.5 %all-reduce.13.cloned.1.call-start = ((), (), s32[]{:S(2)}) async-start(), calls=%async_computation.13 | async-start | bytes 8388608 | tf_op jit(solution)/shard_map/psum | solution.py:152
  458.6 91.9 %copy-start.47 = (bf16[512,128]{1,0:T(8,128)(2,1)}, bf16[512,128]{1,0:T(8,128)(2,1)S(1)}, u32[]{:S(2)}) copy-start(bf16[512,128]{1,0:T(8,128)(2,1)S(1)} %all-reduce.20) | copy-start | bytes 393220
  552.5 283.1 %copy-start.14 = (bf16[512,2048]{1,0:T(8,128)(2,1)}, bf16[512,2048]{1,0:T(8,128)(2,1)S(1)}, u32[]{:S(2)}) copy-start(bf16[512,2048]{1,0:T(8,128)(2,1)S(1)} %fusion.31) | copy-start | bytes 6291460
  1137.1 281.6 %all-reduce.17.cloned.1.call-start = ((), (), s32[]{:S(2)}) async-start(), calls=%async_computation.17 | async-start | bytes 8912896 | tf_op jit(solution)/shard_map/psum | solution.py:174
  1305.3 114.4 %copy-start.37 = (bf16[2048,128]{1,0:T(8,128)(2,1)S(1)}, bf16[2048,128]{1,0:T(8,128)(2,1)}, u32[]{:S(2)}) copy-start(bf16[2048,128]{1,0:T(8,128)(2,1)} %param.36) | copy-start | bytes 1572868
  1305.3 267.4 %reduce-scatter.3.cloned.1.call-start = ((), (), s32[]{:S(2)}) async-start(), calls=%async_computation.14 | async-start | bytes 5242880 | tf_op jit(solution)/shard_map/reduce_scatter | solution.py:227
  1528.1 91.7 %reduce-scatter.5.cloned.1.call-start = ((), (), s32[]{:S(2)}) async-start(), calls=%async_computation.15 | async-start | bytes 5242880 | tf_op jit(solution)/shard_map/reduce_scatter | solution.py:230
  1533.2 185.6 %all-to-all-start.1 = ((bf16[2,256,2048]{2,0,1:T(2,128)(2,1)}), bf16[2,256,2048]{2,0,1:T(2,128)(2,1)}, u32[]{:S(2)}, u32[]{:S(2)}) async-start(bf16[2,256,2048]{2,0,1:T(2,128)(2,1)} %copy.68), calls=%async_computation.1 | async-start | bytes 4194304 | tf_op jit(solution)/shard_map/all_to_all | solution.py:279
  1537.9 167.4 %all-reduce.19.cloned.1.call-start = ((), (), s32[]{:S(2)}) async-start(), calls=%async_computation.18 | async-start | bytes 4980736 | tf_op jit(solution)/shard_map/psum | solution.py:252
  1633.4 360.0 %all-reduce.15.cloned.1.call-start = ((), (), s32[]{:S(2)}) async-start(), calls=%async_computation.16 | async-start | bytes 25165824 | tf_op jit(solution)/shard_map/psum | solution.py:263
  1718.7 76.3 %all-to-all-start.3 = ((bf16[2,256,2048]{2,0,1:T(2,128)(2,1)}), bf16[2,256,2048]{2,0,1:T(2,128)(2,1)S(1)}, u32[]{:S(2)}, u32[]{:S(2)}) async-start(bf16[2,256,2048]{2,0,1:T(2,128)(2,1)} %copy.76), calls=%async_computation.5 | async-start | bytes 4194304 | tf_op jit(solution)/shard_map/all_to_all | solution.py:280
  (84 other events, 574.5 us)
Sparse Core Ops, SparseCore 0:
  9.6 255.7 all-gather.6
  274.7 34.1 all-gather.10
  311.0 35.0 all-gather.8
  347.5 80.7 all-gather.12
  435.2 112.0 all-reduce.10
  548.8 286.7 all-gather.14
  837.2 284.9 all-gather.16
  1137.2 111.6 all-reduce.12
  1305.5 113.2 all-reduce.16
  1528.2 44.4 reduce-scatter.2
  1575.3 44.4 reduce-scatter.4
  1633.6 71.6 all-reduce.18
  1711.8 281.6 all-reduce.14
where the time goes:
time: 2020 us; the launch traced here: 2010 us
  waiting for transfers between devices  1520 us (75%)
  matrix products  235 us (12%)
  local copies, waits for them, and re-layouts  108 us (5%)
  blocking collectives  89.4 us (4%)
  other arithmetic  22 us (1%)
    all_gather x1, waiting for transfers between devices, local(): lax.all_gather(w_up, 'fsdp', axis=0, tiled=True)  276 us
    all_gather x1, waiting for transfers between devices, local(): lax.all_gather(w_down, 'fsdp', axis=1, tiled=True)  266 us
    psum x1, waiting for transfers between devices, local(): lax.psum((grad_a_qkv, grad_b_qkv, grad_a_out, grad_b_out, grad_a_up, grad...  196 us
    all_gather x1, waiting for transfers between devices, local(): lax.all_gather(w_qkv, 'fsdp', axis=1, tiled=True)  141 us
    psum x1, waiting for transfers between devices, local(): lax.psum((part_hidden, part_adapt_up), 'tp')  113 us
    all_to_all x1, waiting for transfers between devices, local(): lax.all_to_all(x_in, 'fsdp', split_axis=0, concat_axis=1, tiled=True)  104 us
    psum x1, waiting for transfers between devices, local(): attn_sum, adapt_out_sum = lax.psum((part_out, part_adapt), 'tp')  88.7 us
    dot_general x18, matrix products, product(): return jnp.dot(left_side, right_side, preferred_element_type=jnp.float32)  86.5 us
  transfers between devices with their start and end apart: 16, of which 15 were waited for; matrix products, arithmetic and copies ran while one was open for 7% of the time, Pallas kernels for 0%

commit v1 on v0

--- a/solution.py
+++ b/solution.py
@@ -10,6 +10,18 @@
 ADAPTERS = 8
 NORM_EPS = 1e-06
 GELU_COEF = 0.7978845608028654
+
+
+def doubled_up(array, axis, dim):
+    ways, here = (lax.axis_size(axis), lax.axis_index(axis))
+    grown, reach = (array, 1)
+    while reach < ways:
+        theirs = lax.ppermute(grown, axis, [(d, d ^ reach) for d in range(ways)])
+        mine_first = jnp.concatenate([grown, theirs], axis=dim)
+        theirs_first = jnp.concatenate([theirs, grown], axis=dim)
+        grown = jnp.where(here & reach == 0, mine_first, theirs_first)
+        reach = 2 * reach
+    return grown
 
 
 def norm_rows(values, gain_row, shift_row):
@@ -140,7 +152,7 @@
     )
     hidden_low = hidden_one.astype(jnp.bfloat16)
     up_full, down_full = (
-        lax.all_gather(w_up, "fsdp", axis=0, tiled=True),
+        doubled_up(w_up, "fsdp", 0),
         lax.all_gather(w_down, "fsdp", axis=1, tiled=True),
     )
     adapt_up = (product(hidden_low, a_up) * pick_rows).astype(jnp.bfloat16)

time: 2020 us -> 2330 us (1.15)
  waiting for transfers between devices: 1520 us -> 1840 us
    ppermute x0 -> x2, waiting for transfers between devices: none -> 700 us  [doubled_up(): theirs = lax.ppermute(grown, axis, [(d, d ^ reach) for d in range(ways)])]
    all_gather x1, waiting for transfers between devices: 266 us -> 0.01 us  [local(): lax.all_gather(w_down, 'fsdp', axis=1, tiled=True)]
    psum x1, waiting for transfers between devices: 88.7 us -> 0.02 us  [local(): attn_sum, adapt_out_sum = lax.psum((part_out, part_adapt), 'tp')]
    all_gather x1, waiting for transfers between devices: 276 us -> 244 us  [local(): lax.all_gather(w_up, 'fsdp', axis=0, tiled=True)]
  transfers between devices with their start and end apart: 16 -> 18, of which waited for: 15 -> 15; matrix products, arithmetic and copies ran while one was open for 7% -> 9% of each run, Pallas kernels for 0% -> 0%
where the time goes in v1:
time: 2330 us
  waiting for transfers between devices  1840 us (79%)
  matrix products  233 us (10%)
  local copies, waits for them, and re-layouts  108 us (5%)
  blocking collectives  83.2 us (4%)
  other arithmetic  33.2 us (1%)
    ppermute x2, waiting for transfers between devices, doubled_up(): theirs = lax.ppermute(grown, axis, [(d, d ^ reach) for d in range(ways)])  700 us
    all_gather x1, waiting for transfers between devices, local(): lax.all_gather(w_up, 'fsdp', axis=0, tiled=True)  244 us
    psum x1, waiting for transfers between devices, local(): lax.psum((grad_a_qkv, grad_b_qkv, grad_a_out, grad_b_out, grad_a_up, grad...  196 us
    all_gather x1, waiting for transfers between devices, local(): lax.all_gather(w_qkv, 'fsdp', axis=1, tiled=True)  141 us
    psum x1, waiting for transfers between devices, local(): lax.psum((part_hidden, part_adapt_up), 'tp')  112 us
    all_to_all x1, waiting for transfers between devices, local(): lax.all_to_all(x_in, 'fsdp', split_axis=0, concat_axis=1, tiled=True)  104 us
    dot_general x18, matrix products, against(): lax.dot_general(left_side, right_side, (((1,), (1,)), ((), ())), preferre...  83.5 us
    dot_general x18, matrix products, product(): return jnp.dot(left_side, right_side, preferred_element_type=jnp.float32)  81.9 us
  transfers between devices with their start and end apart: 18, of which 15 were waited for; matrix products, arithmetic and copies ran while one was open for 9% of the time, Pallas kernels for 0%

profile of v1, /device:TPU:0, one launch (start us, length us, event | category | flops | bytes accessed | tf_op | source)
XLA Modules:
  0.0 2326.2 jit_solution(11973201563506646407)
XLA Ops:
  14.6 104.2 %all-to-all-done = bf16[8,64,2048]{2,1,0:T(8,128)(2,1)S(1)} async-done(((bf16[8,64,2048]{2,1,0:T(8,128)(2,1)}), bf16[8,64,2048]{2,1,0:T(8,128)(2,1)S(1)}, u32[]{:S(2)}, u32[]{:S(2)}) %all-to-all-start) | async-done | bytes 2097184 | tf_op jit(solution)/shard_map/all_to_all | solution.py:87
  124.0 141.4 %all-gather.7.cloned.1.call-done = bf16[3,2048,1024]{2,1,0:T(8,128)(2,1)} async-done(((bf16[3,512,1024]{2,1,0:T(8,128)(2,1)}), bf16[3,2048,1024]{2,1,0:T(8,128)(2,1)}) %all-gather.7.cloned.1.call-update) | async-done | bytes 12582928 | tf_op jit(solution)/shard_map/all_gather | solution.py:101
  297.6 11.3 all-gather.11.cloned.1.call-done
  308.8 37.2 %all-gather.9.cloned.1.call-done = bf16[2,1024,1024]{1,2,0:T(8,128)(2,1)} async-done(((bf16[2,256,1024]{1,2,0:T(8,128)(2,1)}), bf16[2,1024,1024]{1,2,0:T(8,128)(2,1)}) %all-gather.9.cloned.1.call-update) | async-done | bytes 4194320 | tf_op jit(solution)/shard_map/all_gather | solution.py:117
  347.1 26.9 %while.26 = (s32[]{:T(128)}, bf16[2,256,1024]{2,1,0:T(8,128)(2,1)}, f32[2,8,256]{2,1,0:T(8,128)S(1)}, bf16[2,1024,1024]{1,2,0:T(8,128)(2,1)}, pred[2,1024]{1,0:T...) while((s32[]{:T(128)}, bf16[2,256,1024]{2,1,0:T(8,128)(2,1)}, ...), condition=%wide.region_3.4_spmd, body=%wide.region_0.3_spmd.sunk | while | flops 1097070592 | bytes 46208640 | solution.py:142
  374.1 54.2 %all-gather.13.cloned.1.call-done = bf16[1024,2048]{1,0:T(8,128)(2,1)} async-done(((bf16[1024,512]{1,0:T(8,128)(2,1)}), bf16[1024,2048]{1,0:T(8,128)(2,1)}) %all-gather.13.cloned.1.call-update) | async-done | bytes 4194320 | tf_op jit(solution)/shard_map/all_gather | solution.py:102
  435.8 92.6 %collective-permute-done = bf16[512,4096]{1,0:T(8,128)(2,1)} collective-permute-done((bf16[512,4096]{1,0:T(8,128)(2,1)}, bf16[512,4096]{1,0:T(8,128)(2,1)}, u32[]{:S(2)}, u32[]{:S(2)}) %collective-permute-start) | collective-permute-done | bytes 4194336 | tf_op jit(solution)/shard_map/ppermute | solution.py:19
  542.9 13.3 all-reduce.20
  564.3 607.3 %collective-permute-done.1 = bf16[1024,4096]{1,0:T(8,128)(2,1)} collective-permute-done((bf16[1024,4096]{1,0:T(8,128)(2,1)}, bf16[1024,4096]{1,0:T(8,128)(2,1)}, u32[]{:S(2)}, u32[]{:S(2)}) %collective-permute-start.1) | collective-permute-done | bytes 8388640 | tf_op jit(solution)/shard_map/ppermute | solution.py:19
  1171.6 19.7 multiply_convert_fusion.1
  1191.3 15.0 fusion.112
  1207.9 51.1 %all_to_all.60 = bf16[8,64,2048]{2,1,0:T(8,128)(2,1)S(1)} all-to-all(bf16[8,64,2048]{2,1,0:T(8,128)(2,1)S(1)} %copy-done.38), channel_id=1, replica_groups=mesh['fsdp'=4,'ctx'=4,'tp'=2] {'fsdp'}, dimensions={0} | all-to-all | bytes 4194304 | tf_op jit(solution)/shard_map/all_to_all | solution.py:88
  1263.9 18.8 all-reduce.21
  1282.7 35.3 %all-reduce.13.cloned.1.call-done = f32[512,2048]{1,0:T(8,128)} async-done(((f32[512,2048]{1,0:T(8,128)}), f32[512,2048]{1,0:T(8,128)}) %all-reduce.13.cloned.1.call-update) | async-done | bytes 4194320 | tf_op jit(solution)/shard_map/psum | solution.py:164
  1334.4 23.2 fusion.29
  1361.8 244.0 %all-gather.17.cloned.1.call-done = bf16[2048,4096]{1,0:T(8,128)(2,1)} async-done(((bf16[512,4096]{1,0:T(8,128)(2,1)}), bf16[2048,4096]{1,0:T(8,128)(2,1)}) %all-gather.17.cloned.1.call-update) | async-done | bytes 16777232 | tf_op jit(solution)/shard_map/all_gather | solution.py:174
  1605.8 15.5 fusion.114
  1621.4 112.2 %all-reduce.17.cloned.1.call-done = (f32[512,2048]{1,0:T(8,128)}, f32[512,128]{1,0:T(8,128)}) async-done(((f32[512,2048]{1,0:T(8,128)}, f32[512,128]{1,0:T(8,128)}), (f32[512,2048]{1,0:T(8,128)}, f32[512,128]{1,0:T(8,128)})) %all-reduce.17.cloned.1.call-update) | async-done | bytes 4456464 | tf_op jit(solution)/shard_map/psum | solution.py:186
  1751.3 91.5 %while.27 = (s32[]{:T(128)}, bf16[2,256,1024]{2,1,0:T(8,128)(2,1)}, bf16[2,1024,1024]{2,1,0:T(8,128)(2,1)}, bf16[2,1024,1024]{2,1,0:T(8,128)(2,1)}, bf16[2,1024,...) while((s32[]{:T(128)}, bf16[2,256,1024]{2,1,0:T(8,128)(2,1)}, ...), condition=%wide.region_20.21_spmd, body=%wide.region_18.20_spmd.sunk | while | flops 2718431232 | bytes 173603120 | solution.py:235
  1860.2 27.3 %reduce-scatter.3.cloned.1.call-done = bf16[2,256,1024]{2,1,0:T(8,128)(2,1)} async-done(((bf16[2,1024,1024]{2,1,0:T(8,128)(2,1)}), bf16[2,256,1024]{2,1,0:T(8,128)(2,1)}) %reduce-scatter.3.cloned.1.call-update) | async-done | bytes 1048592 | tf_op jit(solution)/shard_map/reduce_scatter | solution.py:239
  1889.1 45.4 %reduce-scatter.5.cloned.1.call-done = bf16[2,256,1024]{2,1,0:T(8,128)(2,1)} async-done(((bf16[2,1024,1024]{2,1,0:T(8,128)(2,1)}), bf16[2,256,1024]{2,1,0:T(8,128)(2,1)}) %reduce-scatter.5.cloned.1.call-update) | async-done | bytes 1048592 | tf_op jit(solution)/shard_map/reduce_scatter | solution.py:242
  1963.7 56.3 %all-reduce.19.cloned.1.call-done = (bf16[3,512,128]{2,1,0:T(8,128)(2,1)}, bf16[512,2048]{1,0:T(8,128)(2,1)}) async-done(((bf16[3,512,128]{2,1,0:T(8,128)(2,1)}, bf16[512,2048]{1,0:T(8,128)(2,1)}), (bf16[3,512,128]{2,1,0:T(8,128)(2,1)}, bf16[512,2048]{1,0:T(8,128)(2,1)})) %all-reduce.19.cloned.1.call-update) | async-done | bytes 2490384 | tf_op jit(solution)/shard_map/psum | solution.py:264
  2041.9 67.8 %all-to-all-done.3 = bf16[2,256,2048]{2,0,1:T(2,128)(2,1)S(1)} async-done(((bf16[2,256,2048]{2,0,1:T(2,128)(2,1)}), bf16[2,256,2048]{2,0,1:T(2,128)(2,1)S(1)}, u32[]{:S(2)}, u32[]{:S(2)}) %all-to-all-start.3) | async-done | bytes 2097184 | tf_op jit(solution)/shard_map/all_to_all | solution.py:292
  2112.0 196.2 %all-reduce.15.cloned.1.call-done = (f32[3,2048,128]{1,2,0:T(8,128)}, f32[3,128,1024]{2,1,0:T(8,128)}, f32[1024,128]{1,0:T(8,128)}, f32[128,2048]{1,0:T(8,128)},...) async-done(((f32[3,2048,128]{1,2,0:T(8,128)}, f32[3,128,1024]{2,1,0:T(8,128)}, f32[1024,128]{1,0:T(8,128)}, ...) | async-done | bytes 12582928 | tf_op jit(solution)/shard_map/psum | solution.py:275
  (372 shorter events, 321.4 us)
Async XLA Ops:
  7.2 1254.4 %copy-start = (bf16[4096,128]{1,0:T(8,128)(2,1)S(1)}, bf16[4096,128]{1,0:T(8,128)(2,1)}, u32[]{:S(2)}) copy-start(bf16[4096,128]{1,0:T(8,128)(2,1)} %param.38) | copy-start | bytes 3145732
  7.2 258.2 %all-gather.7.cloned.1.call-start = ((), (), s32[]{:S(2)}) async-start(), calls=%async_computation.6 | async-start | bytes 15728640 | tf_op jit(solution)/shard_map/all_gather | solution.py:101
  7.9 110.8 %all-to-all-start = ((bf16[8,64,2048]{2,1,0:T(8,128)(2,1)}), bf16[8,64,2048]{2,1,0:T(8,128)(2,1)S(1)}, u32[]{:S(2)}, u32[]{:S(2)}) async-start(bf16[8,64,2048]{2,1,0:T(8,128)(2,1)} %param.22), calls=%async_computation | async-start | bytes 4194304 | tf_op jit(solution)/shard_map/all_to_all | solution.py:87
  14.3 294.6 %all-gather.11.cloned.1.call-start = ((), (), s32[]{:S(2)}) async-start(), calls=%async_computation.8 | async-start | bytes 5242880 | tf_op jit(solution)/shard_map/all_gather | solution.py:116
  14.6 1728.1 %copy-start.70 = (f32[2,128]{1,0:T(2,128)}, f32[2,128]{1,0:T(2,128)S(1)}, u32[]{:S(2)}) copy-start(f32[2,128]{1,0:T(2,128)S(1)} %reshape.257) | copy-start | bytes 3076
  121.8 434.5 %copy-start.6 = (bf16[4,2,64,2048]{3,2,0,1:T(8,128)(2,1)}, bf16[4,2,64,2048]{3,2,0,1:T(8,128)(2,1)S(1)}, u32[]{:S(2)}) copy-start(bf16[4,2,64,2048]{3,2,0,1:T(8,128)(2,1)S(1)} %copy.63) | copy-start | bytes 6291460
  124.0 145.9 %copy-start.52 = (bf16[512,128]{1,0:T(8,128)(2,1)}, bf16[512,128]{1,0:T(8,128)(2,1)S(1)}, u32[]{:S(2)}) copy-start(bf16[512,128]{1,0:T(8,128)(2,1)S(1)} %fusion.42) | copy-start | bytes 393220
  274.5 71.5 %all-gather.9.cloned.1.call-start = ((), (), s32[]{:S(2)}) async-start(), calls=%async_computation.7 | async-start | bytes 5242880 | tf_op jit(solution)/shard_map/all_gather | solution.py:117
  285.6 142.6 %all-gather.13.cloned.1.call-start = ((), (), s32[]{:S(2)}) async-start(), calls=%async_computation.9 | async-start | bytes 5242880 | tf_op jit(solution)/shard_map/all_gather | solution.py:102
  286.2 270.1 %all-reduce.11.cloned.1.call-start = ((), (), s32[]{:S(2)}) async-start(), calls=%async_computation.10 | async-start | bytes 8388608 | tf_op jit(solution)/shard_map/psum | solution.py:146
  435.1 756.2 %all-gather.15.cloned.1.call-start = ((), (), s32[]{:S(2)}) async-start(), calls=%async_computation.11 | async-start | bytes 20971520 | tf_op jit(solution)/shard_map/all_gather | solution.py:156
  435.7 882.4 %all-reduce.13.cloned.1.call-start = ((), (), s32[]{:S(2)}) async-start(), calls=%async_computation.12 | async-start | bytes 8388608 | tf_op jit(solution)/shard_map/psum | solution.py:164
  435.7 92.7 %collective-permute-start = (bf16[512,4096]{1,0:T(8,128)(2,1)}, bf16[512,4096]{1,0:T(8,128)(2,1)}, u32[]{:S(2)}, u32[]{:S(2)}) collective-permute-start(bf16[512,4096]{1,0:T(8,128)(2,1)} %param.28), channel_id=1, source_target_pairs={{0,8},{8,0},{16,24},{24,16},{1,9},{9,1},{17,25},{25,17},{2,10},{10... | collective-permute-start | bytes 12582920 | tf_op jit(solution)/shard_map/ppermute | solution.py:19
  539.6 632.0 %collective-permute-start.1 = (bf16[1024,4096]{1,0:T(8,128)(2,1)}, bf16[1024,4096]{1,0:T(8,128)(2,1)}, u32[]{:S(2)}, u32[]{:S(2)}) collective-permute-start(bf16[1024,4096]{1,0:T(8,128)(2,1)} %maximum_select_fusion.2), channel_id=1, source_target_pairs={{0,16},{8,24},{16,0},{24,8},{1,17},{9,25},{17,1},{25,9},{2,18},{10... | collective-permute-start | bytes 25165832 | tf_op jit(solution)/shard_map/ppermute | solution.py:19
  562.0 609.6 %copy-start.14 = (bf16[512,2048]{1,0:T(8,128)(2,1)}, bf16[512,2048]{1,0:T(8,128)(2,1)S(1)}, u32[]{:S(2)}) copy-start(bf16[512,2048]{1,0:T(8,128)(2,1)S(1)} %fusion.39) | copy-start | bytes 6291460
  1206.3 399.5 %all-gather.17.cloned.1.call-start = ((), (), s32[]{:S(2)}) async-start(), calls=%async_computation.13 | async-start | bytes 20971520 | tf_op jit(solution)/shard_map/all_gather | solution.py:174
  1207.1 526.5 %all-reduce.17.cloned.1.call-start = ((), (), s32[]{:S(2)}) async-start(), calls=%async_computation.17 | async-start | bytes 8912896 | tf_op jit(solution)/shard_map/psum | solution.py:186
  1621.3 113.2 %copy-start.36 = (bf16[2048,128]{1,0:T(8,128)(2,1)S(1)}, bf16[2048,128]{1,0:T(8,128)(2,1)}, u32[]{:S(2)}) copy-start(bf16[2048,128]{1,0:T(8,128)(2,1)} %param.36) | copy-start | bytes 1572868
  1621.4 266.1 %reduce-scatter.3.cloned.1.call-start = ((), (), s32[]{:S(2)}) async-start(), calls=%async_computation.14 | async-start | bytes 5242880 | tf_op jit(solution)/shard_map/reduce_scatter | solution.py:239
  1842.8 91.8 %reduce-scatter.5.cloned.1.call-start = ((), (), s32[]{:S(2)}) async-start(), calls=%async_computation.15 | async-start | bytes 5242880 | tf_op jit(solution)/shard_map/reduce_scatter | solution.py:242
  1847.8 185.7 %all-to-all-start.1 = ((bf16[2,256,2048]{2,0,1:T(2,128)(2,1)}), bf16[2,256,2048]{2,0,1:T(2,128)(2,1)}, u32[]{:S(2)}, u32[]{:S(2)}) async-start(bf16[2,256,2048]{2,0,1:T(2,128)(2,1)} %copy.68), calls=%async_computation.1 | async-start | bytes 4194304 | tf_op jit(solution)/shard_map/all_to_all | solution.py:291
  1852.5 167.5 %all-reduce.19.cloned.1.call-start = ((), (), s32[]{:S(2)}) async-start(), calls=%async_computation.18 | async-start | bytes 4980736 | tf_op jit(solution)/shard_map/psum | solution.py:264
  1948.2 360.0 %all-reduce.15.cloned.1.call-start = ((), (), s32[]{:S(2)}) async-start(), calls=%async_computation.16 | async-start | bytes 25165824 | tf_op jit(solution)/shard_map/psum | solution.py:275
  2033.5 76.3 %all-to-all-start.3 = ((bf16[2,256,2048]{2,0,1:T(2,128)(2,1)}), bf16[2,256,2048]{2,0,1:T(2,128)(2,1)S(1)}, u32[]{:S(2)}, u32[]{:S(2)}) async-start(bf16[2,256,2048]{2,0,1:T(2,128)(2,1)} %copy.76), calls=%async_computation.5 | async-start | bytes 4194304 | tf_op jit(solution)/shard_map/all_to_all | solution.py:292
  (87 other events, 955.1 us)
Sparse Core Ops, SparseCore 0:
  9.6 255.7 all-gather.6
  274.7 34.1 all-gather.10
  311.0 35.0 all-gather.8
  347.5 80.7 all-gather.12
  435.2 106.3 all-reduce.10
  543.1 583.8 all-gather.14
  1206.4 111.5 all-reduce.12
  1319.6 286.1 all-gather.16
  1621.5 112.0 all-reduce.16
  1842.9 44.5 reduce-scatter.2
  1890.0 44.5 reduce-scatter.4
  1948.3 71.6 all-reduce.18
  2026.5 281.6 all-reduce.14
